TPU v7x, 32 devices: a whole 2x2x4 slice. The times are simulated.
32 devices in a mesh: grp: 2 (over y), tr: 8 (over z, x), root: 2 (over core).
Axes of the slice: x: 2, y: 2, z: 4, core: 2. Of those that a mesh axis runs over, the one named last changes fastest.
Arguments:
- residual: bfloat16 [128, 65536], P('root', ('grp', 'tr')), parts along dimension 1, may hold values from -8 to 8
- subspace: bfloat16 [512, 65536], P(None, ('grp', 'tr')), parts along dimension 1, may hold values from -1 to 1, as said below
- inverses: bfloat16 [16, 512, 512], P(('grp', 'tr')), parts along dimension 0, may hold values from -1 to 3, as said below
- owner_offset: int32 [128], P(('grp', 'tr')), parts along dimension 0, may hold values from 0 to 3, as said below
- listed: int32 [128], P(('grp', 'tr')), parts along dimension 0, may hold values from 0 to 1, as said below
Outputs:
- corrections: float32 [128, 65536], P('root', ('grp', 'tr')), parts along dimension 1
There are 2 independent parts, one for each index of `grp`. A program takes and returns all parts, laid end to end along the dimension named above; each array names one. Nothing has to cross between parts.
Inputs may be any that keep to these rules, and one draw needn't show every extreme that they name: Each entry of subspace lies within the stated range; rows are not normalized. `inverses`: each inverse is a dense real matrix. `owner_offset`: among the 8 blocks of each shard, at least one is listed and has offset 3. Each shard has at least one listed block and at least one unlisted block.
All inputs are finite; a program needn't handle non-finite values.
Results may differ from a plain program's by a relative error of at most 0.0065.
Values may be sent and summed in bfloat16 or wider, within the bound.
A program may use at most 64 MiB of HBM per device.

v0:
```python
import jax
import jax.numpy as jnp
from jax import lax
from jax.sharding import PartitionSpec as P

BLK = 512
OFFS = 4
PASSES = 2


def from_behind(block, axis, distance):
    devices = range(lax.axis_size(axis))
    route = [((i - distance) % len(devices), i) for i in devices]
    return lax.ppermute(block, axis, route)


def per_device(residual, subspace, inverses, owner_offset, listed):
    root_count, row_count = residual.shape
    block_count = row_count // BLK
    blocks = residual.reshape(root_count, block_count, BLK)
    chosen_mask = listed > 0
    inverse = inverses[0]
    target = jnp.arange(OFFS, dtype=jnp.int32)
    held_inverses = [inverse]
    for offset in range(1, OFFS):
        held_inverses.append(from_behind(inverse, "tr", -offset))
    inverse_table = jnp.stack(held_inverses)
    selector = (owner_offset[:, None] == target[None, :]).astype(jnp.bfloat16)
    picked = jnp.einsum(
        "jd,dbc->jbc", selector, inverse_table, preferred_element_type=jnp.float32
    ).astype(jnp.bfloat16)
    solved = jnp.einsum("rjb,jbc->rjc", blocks, picked, preferred_element_type=jnp.float32)
    precond = jnp.where(chosen_mask[None, :, None], solved, blocks.astype(jnp.float32)).reshape(
        root_count, row_count
    )
    current = precond
    for repeat in range(PASSES):
        rounded = current.astype(jnp.bfloat16)
        partial_correlation = lax.dot_general(
            rounded, subspace, (((1,), (1,)), ((), ())), preferred_element_type=jnp.float32
        )
        correlation = lax.psum(partial_correlation, "tr")
        coefficients = correlation.astype(jnp.bfloat16)
        current = current - jnp.dot(coefficients, subspace, preferred_element_type=jnp.float32)
    return current


def solution(mesh):
    return jax.shard_map(
        per_device,
        mesh=mesh,
        in_specs=(
            P("root", ("grp", "tr")),
            P(None, ("grp", "tr")),
            P(("grp", "tr"), None, None),
            P(("grp", "tr")),
            P(("grp", "tr")),
        ),
        out_specs=P("root", ("grp", "tr")),
        check_vma=False,
    )
```

profile of v0, /device:TPU:0, one launch (start us, length us, event | category | flops | bytes accessed | tf_op | source)
XLA Modules:
  0.0 140.2 jit_solution(10332493646921314701)
XLA Ops:
  0.0 6.0 %collective-permute-start = (bf16[512,512]{1,0:T(8,128)(2,1)}, bf16[512,512]{1,0:T(8,128)(2,1)S(1)}, u32[]{:S(2)}, u32[]{:S(2)}) collective-permute-start(bf16[512,512]{1,0:T(8,128)(2,1)} %bitcast.28), channel_id=1, source_target_pairs={{2,0},{4,2},{6,4},{8,6},{10,8},{12,10},{14,12},{0,14},{3,1},{5,3},... | collective-permute-start | bytes 1572872 | tf_op jit(solution)/shard_map/ppermute | solution.py:14
  6.0 0.4 collective-permute-start.1
  6.5 0.0 collective-permute-start.2
  6.5 0.7 broadcast_compare_fusion
  7.1 11.6 %collective-permute-done = bf16[512,512]{1,0:T(8,128)(2,1)S(1)} collective-permute-done((bf16[512,512]{1,0:T(8,128)(2,1)}, bf16[512,512]{1,0:T(8,128)(2,1)S(1)}, u32[]{:S(2)}, u32[]{:S(2)}) %collective-permute-start) | collective-permute-done | bytes 524320 | tf_op jit(solution)/shard_map/ppermute | solution.py:14
  18.7 11.2 %collective-permute-done.1 = bf16[512,512]{1,0:T(8,128)(2,1)S(1)} collective-permute-done((bf16[512,512]{1,0:T(8,128)(2,1)}, bf16[512,512]{1,0:T(8,128)(2,1)S(1)}, u32[]{:S(2)}, u32[]{:S(2)}) %collective-permute-start.1) | collective-permute-done | bytes 524320 | tf_op jit(solution)/shard_map/ppermute | solution.py:14
  29.9 10.1 %collective-permute-done.2 = bf16[512,512]{1,0:T(8,128)(2,1)S(1)} collective-permute-done((bf16[512,512]{1,0:T(8,128)(2,1)}, bf16[512,512]{1,0:T(8,128)(2,1)S(1)}, u32[]{:S(2)}, u32[]{:S(2)}) %collective-permute-start.2) | collective-permute-done | bytes 524320 | tf_op jit(solution)/shard_map/ppermute | solution.py:14
  40.0 1.3 pad_maximum_fusion
  41.3 0.0 copy-done.2
  41.3 0.0 copy-start.3
  41.3 1.5 %fusion.1 = bf16[8,512,512]{2,0,1:T(8,128)(2,1)S(1)} fusion(bf16[4,512,512]{2,1,0:T(8,128)(2,1)S(1)} %pad_maximum_fusion, s32[8]{0:T(128)S(1)} %copy-done.2), kind=kOutput, calls=%fused_computation.5 | convolution fusion | flops 16777248 | bytes 6291488 | tf_op jit(solution)/shard_map/jd,dbc->jbc/dot_general | solution.py:29
  42.9 0.0 copy-done.3
  42.9 0.0 copy-start
  42.9 2.5 %fusion.5 = f32[8,8,8,512]{3,2,1,0:T(8,128)S(1)} fusion(bf16[8,512,512]{2,0,1:T(8,128)(2,1)S(1)} %fusion.1, bf16[8,8,8,512]{3,2,1,0:T(8,128)(2,1)S(1)} %bitcast.34, pred[8]{0:T(512)(128)(4,1)S(1)} %broadcast_compare_fusion), kind=kOutput, calls=%fused_computation.9 | convolution fusion | flops 268959744 | bytes 5767176 | tf_op jit(solution)/shard_map/rjb,jbc->rjc/dot_general | solution.py:32
  45.4 0.1 copy.12
  45.4 0.0 copy-done
  45.5 1.4 %fusion.10 = f32[64,512]{1,0:T(8,128)S(1)} fusion(bf16[512,4096]{1,0:T(8,128)(2,1)S(1)} %copy-done, f32[64,4096]{1,0:T(8,128)S(1)} %bitcast.26), kind=kOutput, calls=%fused_computation.14 | convolution fusion | flops 268697600 | bytes 5373952 | tf_op jit(solution)/shard_map/dot_general | solution.py:39
  46.9 50.4 %all-reduce.2 = bf16[64,512]{1,0:T(8,128)(2,1)S(1)} all-reduce(f32[64,512]{1,0:T(8,128)S(1)} %fusion.10), channel_id=1, replica_groups=mesh['grp'=2,'tr'=8,'root'=2] {'tr'}, use_global_device_ids=true, to_apply=%region_0.1 | all-reduce | flops 32768 | bytes 196608 | tf_op jit(solution)/shard_map/psum | solution.py:42
  97.2 0.0 copy-start.1
  97.2 3.2 %convolution_subtract_fusion.1 = f32[64,4096]{1,0:T(8,128)S(1)} fusion(f32[64,4096]{1,0:T(8,128)S(1)} %bitcast.27, bf16[512,4096]{1,0:T(8,128)(2,1)} %param.6, bf16[64,512]{1,0:T(8,128)(2,1)S(1)} %all-reduce.2), kind=kOutput, calls=%fused_computation.2 | convolution fusion | flops 268697600 | bytes 6356992 | tf_op jit(solution)/shard_map/dot_general | solution.py:44
  100.4 0.3 copy-done.1
  100.7 1.4 fusion.8
  102.1 34.1 %all-reduce.3 = bf16[64,512]{1,0:T(8,128)(2,1)S(1)} all-reduce(f32[64,512]{1,0:T(8,128)S(1)} %fusion.8), channel_id=1, replica_groups=mesh['grp'=2,'tr'=8,'root'=2] {'tr'}, use_global_device_ids=true, to_apply=%region_1.2 | all-reduce | flops 32768 | bytes 196608 | tf_op jit(solution)/shard_map/psum | solution.py:42
  136.2 4.0 %convolution_subtract_fusion = f32[64,4096]{1,0:T(8,128)} fusion(f32[64,4096]{1,0:T(8,128)S(1)} %convolution_subtract_fusion.1, bf16[512,4096]{1,0:T(8,128)(2,1)} %param.6, bf16[64,512]{1,0:T(8,128)(2,1)S(1)} %all-reduce.3), kind=kOutput, calls=%fused_computation.1 | convolution fusion | flops 268697600 | bytes 6356992 | tf_op jit(solution)/shard_map/dot_general | solution.py:44
  (1 shorter events, 0.0 us)
Async XLA Ops:
  0.0 41.3 %copy-start.2 = (s32[8]{0:T(128)S(1)}, s32[8]{0:T(128)}, u32[]{:S(2)}) copy-start(s32[8]{0:T(128)} %param.8) | copy-start | bytes 100
  0.0 18.7 %collective-permute-start = (bf16[512,512]{1,0:T(8,128)(2,1)}, bf16[512,512]{1,0:T(8,128)(2,1)S(1)}, u32[]{:S(2)}, u32[]{:S(2)}) collective-permute-start(bf16[512,512]{1,0:T(8,128)(2,1)} %bitcast.28), channel_id=1, source_target_pairs={{2,0},{4,2},{6,4},{8,6},{10,8},{12,10},{14,12},{0,14},{3,1},{5,3},... | collective-permute-start | bytes 1572872 | tf_op jit(solution)/shard_map/ppermute | solution.py:14
  6.0 23.9 %collective-permute-start.1 = (bf16[512,512]{1,0:T(8,128)(2,1)}, bf16[512,512]{1,0:T(8,128)(2,1)S(1)}, u32[]{:S(2)}, u32[]{:S(2)}) collective-permute-start(bf16[512,512]{1,0:T(8,128)(2,1)} %bitcast.29), channel_id=1, source_target_pairs={{4,0},{6,2},{8,4},{10,6},{12,8},{14,10},{0,12},{2,14},{5,1},{7,3},... | collective-permute-start | bytes 1572872 | tf_op jit(solution)/shard_map/ppermute | solution.py:14
  6.5 33.6 %collective-permute-start.2 = (bf16[512,512]{1,0:T(8,128)(2,1)}, bf16[512,512]{1,0:T(8,128)(2,1)S(1)}, u32[]{:S(2)}, u32[]{:S(2)}) collective-permute-start(bf16[512,512]{1,0:T(8,128)(2,1)} %bitcast.30), channel_id=1, source_target_pairs={{6,0},{8,2},{10,4},{12,6},{14,8},{0,10},{2,12},{4,14},{7,1},{9,3},... | collective-permute-start | bytes 1572872 | tf_op jit(solution)/shard_map/ppermute | solution.py:14
  41.3 1.5 %copy-start.3 = (bf16[64,4096]{1,0:T(8,128)(2,1)S(1)}, bf16[64,4096]{1,0:T(8,128)(2,1)}, u32[]{:S(2)}) copy-start(bf16[64,4096]{1,0:T(8,128)(2,1)} %param.5) | copy-start | bytes 1572868
  42.9 2.6 %copy-start = (bf16[512,4096]{1,0:T(8,128)(2,1)S(1)}, bf16[512,4096]{1,0:T(8,128)(2,1)}, u32[]{:S(2)}) copy-start(bf16[512,4096]{1,0:T(8,128)(2,1)} %param.6) | copy-start | bytes 12582916
  97.2 3.5 %copy-start.1 = (bf16[512,4096]{1,0:T(8,128)(2,1)S(1)}, bf16[512,4096]{1,0:T(8,128)(2,1)}, u32[]{:S(2)}) copy-start(bf16[512,4096]{1,0:T(8,128)(2,1)} %param.6) | copy-start | bytes 12582916
where the time goes:
time: 140 us
  blocking collectives  84.5 us (60%)
  waiting for transfers between devices  32.9 us (24%)
  matrix products  14 us (10%)
  starting transfers between devices  6.46 us (5%)
  other arithmetic  1.96 us (1%)
    psum x2, blocking collectives, per_device(): correlation = lax.psum(partial_correlation, 'tr')  84.5 us
    ppermute x3, waiting for transfers between devices, from_behind(): return lax.ppermute(block, axis, route)  32.9 us
    dot_general x2, matrix products, per_device(): jnp.dot(coefficients, subspace, preferred_element_type=jnp.float32)  7.19 us
    ppermute x3, starting transfers between devices, from_behind(): return lax.ppermute(block, axis, route)  6.46 us
    dot_general x2, matrix products, per_device(): lax.dot_general(rounded, subspace, (((1,), (1,)), ((), ())), preferred_el...  2.8 us
  transfers between devices with their start and end apart: 3, of which 3 were waited for; matrix products, arithmetic and copies ran while one was open for 0% of the time, Pallas kernels for 0%

commit v1 on v0

--- a/solution.py
+++ b/solution.py
@@ -6,6 +6,14 @@
 BLK = 512
 OFFS = 4
 PASSES = 2
+
+
+def steps_all_work(block_in):
+    ndev = lax.axis_size("tr")
+    t1 = block_in
+    for at in [k for k in (1, 2, 4, 8, 16) if k < ndev]:
+        t1 = t1 + lax.ppermute(t1, axis_name="tr", perm=[(to_i, to_i ^ at) for to_i in range(ndev)])
+    return t1
 
 
 def from_behind(block, axis, distance):
@@ -39,7 +47,7 @@
         partial_correlation = lax.dot_general(
             rounded, subspace, (((1,), (1,)), ((), ())), preferred_element_type=jnp.float32
         )
-        correlation = lax.psum(partial_correlation, "tr")
+        correlation = steps_all_work(partial_correlation)
         coefficients = correlation.astype(jnp.bfloat16)
         current = current - jnp.dot(coefficients, subspace, preferred_element_type=jnp.float32)
     return current

time: 140 us -> 98.3 us (0.70)
  blocking collectives: 84.5 us -> 0 us
  waiting for transfers between devices: 32.9 us -> 57.7 us
  starting transfers between devices: 6.46 us -> 28.8 us
  matrix products: 14 us -> 9.44 us
    psum x2 -> x0, blocking collectives: 84.5 us -> none  [per_device(): correlation = lax.psum(partial_correlation, 'tr')]
    ppermute x0 -> x6, waiting for transfers between devices: none -> 24.8 us  [steps_all_work(): lax.ppermute(t1, axis_name='tr', perm=[(to_i, to_i ^ at) for to_i in rang...]
    ppermute x0 -> x6, starting transfers between devices: none -> 22.3 us  [steps_all_work(): lax.ppermute(t1, axis_name='tr', perm=[(to_i, to_i ^ at) for to_i in rang...]
    dot_general x2, matrix products: 7.19 us -> 2.66 us  [per_device(): jnp.dot(coefficients, subspace, preferred_element_type=jnp.float32)]
  transfers between devices with their start and end apart: 3 -> 9, of which waited for: 3 -> 9; matrix products, arithmetic and copies ran while one was open for 0% -> 1% of each run, Pallas kernels for 0% -> 0%
where the time goes in v1:
time: 98.3 us; the launch traced here: 98.1 us
  waiting for transfers between devices  57.7 us (59%)
  starting transfers between devices  28.8 us (29%)
  matrix products  9.44 us (10%)
  other arithmetic  2.04 us (2%)
    ppermute x3, waiting for transfers between devices, from_behind(): return lax.ppermute(block, axis, route)  32.9 us
    ppermute x6, waiting for transfers between devices, steps_all_work(): lax.ppermute(t1, axis_name='tr', perm=[(to_i, to_i ^ at) for to_i in rang...  24.8 us
    ppermute x6, starting transfers between devices, steps_all_work(): lax.ppermute(t1, axis_name='tr', perm=[(to_i, to_i ^ at) for to_i in rang...  22.3 us
    ppermute x3, starting transfers between devices, from_behind(): return lax.ppermute(block, axis, route)  6.46 us
    dot_general x2, matrix products, per_device(): lax.dot_general(rounded, subspace, (((1,), (1,)), ((), ())), preferred_el...  2.79 us
    dot_general x2, matrix products, per_device(): jnp.dot(coefficients, subspace, preferred_element_type=jnp.float32)  2.66 us
    dot_general x1, matrix products, per_device(): jnp.einsum('rjb,jbc->rjc', blocks, picked, preferred_element_type=jnp.flo...  2.46 us
  transfers between devices with their start and end apart: 9, of which 9 were waited for; matrix products, arithmetic and copies ran while one was open for 1% of the time, Pallas kernels for 0%

profile of v1, /device:TPU:0, one launch (start us, length us, event | category | flops | bytes accessed | tf_op | source)
XLA Modules:
  0.0 98.1 jit_solution(16321838392906028172)
XLA Ops:
  0.0 6.0 %collective-permute-start = (bf16[512,512]{1,0:T(8,128)(2,1)}, bf16[512,512]{1,0:T(8,128)(2,1)S(1)}, u32[]{:S(2)}, u32[]{:S(2)}) collective-permute-start(bf16[512,512]{1,0:T(8,128)(2,1)} %bitcast.26), channel_id=1, source_target_pairs={{2,0},{4,2},{6,4},{8,6},{10,8},{12,10},{14,12},{0,14},{3,1},{5,3},... | collective-permute-start | bytes 1572872 | tf_op jit(solution)/shard_map/ppermute | solution.py:22
  6.5 0.7 broadcast_compare_fusion
  7.1 11.6 %collective-permute-done = bf16[512,512]{1,0:T(8,128)(2,1)S(1)} collective-permute-done((bf16[512,512]{1,0:T(8,128)(2,1)}, bf16[512,512]{1,0:T(8,128)(2,1)S(1)}, u32[]{:S(2)}, u32[]{:S(2)}) %collective-permute-start) | collective-permute-done | bytes 524320 | tf_op jit(solution)/shard_map/ppermute | solution.py:22
  18.7 11.2 %collective-permute-done.1 = bf16[512,512]{1,0:T(8,128)(2,1)S(1)} collective-permute-done((bf16[512,512]{1,0:T(8,128)(2,1)}, bf16[512,512]{1,0:T(8,128)(2,1)S(1)}, u32[]{:S(2)}, u32[]{:S(2)}) %collective-permute-start.1) | collective-permute-done | bytes 524320 | tf_op jit(solution)/shard_map/ppermute | solution.py:22
  29.9 10.1 %collective-permute-done.2 = bf16[512,512]{1,0:T(8,128)(2,1)S(1)} collective-permute-done((bf16[512,512]{1,0:T(8,128)(2,1)}, bf16[512,512]{1,0:T(8,128)(2,1)S(1)}, u32[]{:S(2)}, u32[]{:S(2)}) %collective-permute-start.2) | collective-permute-done | bytes 524320 | tf_op jit(solution)/shard_map/ppermute | solution.py:22
  40.0 1.3 %pad_maximum_fusion = bf16[4,512,512]{2,1,0:T(8,128)(2,1)S(1)} fusion(bf16[1,512,512]{2,1,0:T(8,128)(2,1)S(1)} %bitcast.31, bf16[1,512,512]{2,1,0:T(8,128)(2,1)S(1)} %bitcast.30, bf16[1,512,512]{2,1,0:T(8,128)(2,1)S(1)} %bitcast.29, bf16[1,512,512]{2,1,0:T(8,128)(2,1)} %param.7), kind=kLoop, calls=%fused_computation.4 | loop fusion | flops 3145728 | bytes 4194304 | tf_op jit(solution)/shard_map/stack | solution.py:35
  41.3 1.5 %fusion.1 = bf16[8,512,512]{2,0,1:T(8,128)(2,1)S(1)} fusion(bf16[4,512,512]{2,1,0:T(8,128)(2,1)S(1)} %pad_maximum_fusion, s32[8]{0:T(128)S(1)} %copy-done.1), kind=kOutput, calls=%fused_computation.5 | convolution fusion | flops 16777248 | bytes 6291488 | tf_op jit(solution)/shard_map/jd,dbc->jbc/dot_general | solution.py:37
  42.9 2.5 %fusion.5 = f32[8,8,8,512]{3,2,1,0:T(8,128)S(1)} fusion(bf16[8,512,512]{2,0,1:T(8,128)(2,1)S(1)} %fusion.1, bf16[8,8,8,512]{3,2,1,0:T(8,128)(2,1)S(1)} %bitcast.32, pred[8]{0:T(512)(128)(4,1)S(1)} %broadcast_compare_fusion), kind=kOutput, calls=%fused_computation.9 | convolution fusion | flops 268959744 | bytes 5767176 | tf_op jit(solution)/shard_map/rjb,jbc->rjc/dot_general | solution.py:40
  45.5 1.4 %fusion.10 = f32[64,512]{1,0:T(8,128)S(1)} fusion(bf16[512,4096]{1,0:T(8,128)(2,1)S(1)} %copy-done, f32[64,4096]{1,0:T(8,128)S(1)} %bitcast.24), kind=kOutput, calls=%fused_computation.14 | convolution fusion | flops 268697600 | bytes 5373952 | tf_op jit(solution)/shard_map/dot_general | solution.py:47
  46.9 12.5 %collective-permute-start.3 = (f32[64,512]{1,0:T(8,128)S(1)}, f32[64,512]{1,0:T(8,128)S(1)}, u32[]{:S(2)}, u32[]{:S(2)}) collective-permute-start(f32[64,512]{1,0:T(8,128)S(1)} %fusion.10), channel_id=1, source_target_pairs={{0,2},{2,0},{4,6},{6,4},{8,10},{10,8},{12,14},{14,12},{1,3},{3,1},... | collective-permute-start | bytes 393224 | tf_op jit(solution)/shard_map/ppermute | solution.py:15
  59.4 2.9 %collective-permute-done.3 = f32[64,512]{1,0:T(8,128)S(1)} collective-permute-done((f32[64,512]{1,0:T(8,128)S(1)}, f32[64,512]{1,0:T(8,128)S(1)}, u32[]{:S(2)}, u32[]{:S(2)}) %collective-permute-start.3) | collective-permute-done | bytes 131104 | tf_op jit(solution)/shard_map/ppermute | solution.py:15
  62.3 2.7 %collective-permute-start.4 = (f32[64,512]{1,0:T(8,128)S(1)}, f32[64,512]{1,0:T(8,128)S(1)}, u32[]{:S(2)}, u32[]{:S(2)}) collective-permute-start(f32[64,512]{1,0:T(8,128)S(1)} %add.18), channel_id=1, source_target_pairs={{0,4},{2,6},{4,0},{6,2},{8,12},{10,14},{12,8},{14,10},{1,5},{3,7},... | collective-permute-start | bytes 393224 | tf_op jit(solution)/shard_map/ppermute | solution.py:15
  65.1 2.9 %collective-permute-done.4 = f32[64,512]{1,0:T(8,128)S(1)} collective-permute-done((f32[64,512]{1,0:T(8,128)S(1)}, f32[64,512]{1,0:T(8,128)S(1)}, u32[]{:S(2)}, u32[]{:S(2)}) %collective-permute-start.4) | collective-permute-done | bytes 131104 | tf_op jit(solution)/shard_map/ppermute | solution.py:15
  68.1 3.2 %collective-permute-start.5 = (f32[64,512]{1,0:T(8,128)S(1)}, f32[64,512]{1,0:T(8,128)S(1)}, u32[]{:S(2)}, u32[]{:S(2)}) collective-permute-start(f32[64,512]{1,0:T(8,128)S(1)} %add.19), channel_id=1, source_target_pairs={{0,8},{2,10},{4,12},{6,14},{8,0},{10,2},{12,4},{14,6},{1,9},{3,11}... | collective-permute-start | bytes 393224 | tf_op jit(solution)/shard_map/ppermute | solution.py:15
  71.3 5.3 %collective-permute-done.5 = f32[64,512]{1,0:T(8,128)S(1)} collective-permute-done((f32[64,512]{1,0:T(8,128)S(1)}, f32[64,512]{1,0:T(8,128)S(1)}, u32[]{:S(2)}, u32[]{:S(2)}) %collective-permute-start.5) | collective-permute-done | bytes 131104 | tf_op jit(solution)/shard_map/ppermute | solution.py:15
  76.6 0.8 convolution_subtract_fusion.1
  77.5 1.4 %fusion.8 = f32[64,512]{1,0:T(8,128)S(1)} fusion(bf16[512,4096]{1,0:T(8,128)(2,1)S(1)} %copy-done, f32[64,4096]{1,0:T(8,128)S(1)} %convolution_subtract_fusion.1), kind=kOutput, calls=%fused_computation.12 | convolution fusion | flops 268697600 | bytes 5373952 | tf_op jit(solution)/shard_map/dot_general | solution.py:47
  78.9 1.1 %collective-permute-start.6 = (f32[64,512]{1,0:T(8,128)S(1)}, f32[64,512]{1,0:T(8,128)S(1)}, u32[]{:S(2)}, u32[]{:S(2)}) collective-permute-start(f32[64,512]{1,0:T(8,128)S(1)} %fusion.8), channel_id=1, source_target_pairs={{0,2},{2,0},{4,6},{6,4},{8,10},{10,8},{12,14},{14,12},{1,3},{3,1},... | collective-permute-start | bytes 393224 | tf_op jit(solution)/shard_map/ppermute | solution.py:15
  79.9 4.0 %collective-permute-done.6 = f32[64,512]{1,0:T(8,128)S(1)} collective-permute-done((f32[64,512]{1,0:T(8,128)S(1)}, f32[64,512]{1,0:T(8,128)S(1)}, u32[]{:S(2)}, u32[]{:S(2)}) %collective-permute-start.6) | collective-permute-done | bytes 131104 | tf_op jit(solution)/shard_map/ppermute | solution.py:15
  83.9 0.6 collective-permute-start.7
  84.5 4.4 %collective-permute-done.7 = f32[64,512]{1,0:T(8,128)S(1)} collective-permute-done((f32[64,512]{1,0:T(8,128)S(1)}, f32[64,512]{1,0:T(8,128)S(1)}, u32[]{:S(2)}, u32[]{:S(2)}) %collective-permute-start.7) | collective-permute-done | bytes 131104 | tf_op jit(solution)/shard_map/ppermute | solution.py:15
  89.0 2.2 %collective-permute-start.8 = (f32[64,512]{1,0:T(8,128)S(1)}, f32[64,512]{1,0:T(8,128)S(1)}, u32[]{:S(2)}, u32[]{:S(2)}) collective-permute-start(f32[64,512]{1,0:T(8,128)S(1)} %add.22), channel_id=1, source_target_pairs={{0,8},{2,10},{4,12},{6,14},{8,0},{10,2},{12,4},{14,6},{1,9},{3,11}... | collective-permute-start | bytes 393224 | tf_op jit(solution)/shard_map/ppermute | solution.py:15
  91.1 5.2 %collective-permute-done.8 = f32[64,512]{1,0:T(8,128)S(1)} collective-permute-done((f32[64,512]{1,0:T(8,128)S(1)}, f32[64,512]{1,0:T(8,128)S(1)}, u32[]{:S(2)}, u32[]{:S(2)}) %collective-permute-start.8) | collective-permute-done | bytes 131104 | tf_op jit(solution)/shard_map/ppermute | solution.py:15
  96.3 1.8 %convolution_subtract_fusion = f32[64,4096]{1,0:T(8,128)} fusion(f32[64,4096]{1,0:T(8,128)S(1)} %convolution_subtract_fusion.1, bf16[512,4096]{1,0:T(8,128)(2,1)S(1)} %copy-done, f32[64,512]{1,0:T(8,128)S(1)} %add.22, f32[64,512]{1,0:T(8,128)S(1)} %collective-permute-done.8), kind=kOutput, calls=%fused_computation.1 | convolution fusion | flops 268763136 | bytes 6553600 | tf_op jit(solution)/shard_map/dot_general | solution.py:52
  (13 shorter events, 0.6 us)
Async XLA Ops:
  0.0 41.3 %copy-start.1 = (s32[8]{0:T(128)S(1)}, s32[8]{0:T(128)}, u32[]{:S(2)}) copy-start(s32[8]{0:T(128)} %param.8) | copy-start | bytes 100
  0.0 18.7 %collective-permute-start = (bf16[512,512]{1,0:T(8,128)(2,1)}, bf16[512,512]{1,0:T(8,128)(2,1)S(1)}, u32[]{:S(2)}, u32[]{:S(2)}) collective-permute-start(bf16[512,512]{1,0:T(8,128)(2,1)} %bitcast.26), channel_id=1, source_target_pairs={{2,0},{4,2},{6,4},{8,6},{10,8},{12,10},{14,12},{0,14},{3,1},{5,3},... | collective-permute-start | bytes 1572872 | tf_op jit(solution)/shard_map/ppermute | solution.py:22
  6.0 23.9 %collective-permute-start.1 = (bf16[512,512]{1,0:T(8,128)(2,1)}, bf16[512,512]{1,0:T(8,128)(2,1)S(1)}, u32[]{:S(2)}, u32[]{:S(2)}) collective-permute-start(bf16[512,512]{1,0:T(8,128)(2,1)} %bitcast.27), channel_id=1, source_target_pairs={{4,0},{6,2},{8,4},{10,6},{12,8},{14,10},{0,12},{2,14},{5,1},{7,3},... | collective-permute-start | bytes 1572872 | tf_op jit(solution)/shard_map/ppermute | solution.py:22
  6.5 33.6 %collective-permute-start.2 = (bf16[512,512]{1,0:T(8,128)(2,1)}, bf16[512,512]{1,0:T(8,128)(2,1)S(1)}, u32[]{:S(2)}, u32[]{:S(2)}) collective-permute-start(bf16[512,512]{1,0:T(8,128)(2,1)} %bitcast.28), channel_id=1, source_target_pairs={{6,0},{8,2},{10,4},{12,6},{14,8},{0,10},{2,12},{4,14},{7,1},{9,3},... | collective-permute-start | bytes 1572872 | tf_op jit(solution)/shard_map/ppermute | solution.py:22
  41.3 1.5 %copy-start.2 = (bf16[64,4096]{1,0:T(8,128)(2,1)S(1)}, bf16[64,4096]{1,0:T(8,128)(2,1)}, u32[]{:S(2)}) copy-start(bf16[64,4096]{1,0:T(8,128)(2,1)} %param.5) | copy-start | bytes 1572868
  42.9 2.6 %copy-start = (bf16[512,4096]{1,0:T(8,128)(2,1)S(1)}, bf16[512,4096]{1,0:T(8,128)(2,1)}, u32[]{:S(2)}) copy-start(bf16[512,4096]{1,0:T(8,128)(2,1)} %param.6) | copy-start | bytes 12582916
  46.9 15.5 %collective-permute-start.3 = (f32[64,512]{1,0:T(8,128)S(1)}, f32[64,512]{1,0:T(8,128)S(1)}, u32[]{:S(2)}, u32[]{:S(2)}) collective-permute-start(f32[64,512]{1,0:T(8,128)S(1)} %fusion.10), channel_id=1, source_target_pairs={{0,2},{2,0},{4,6},{6,4},{8,10},{10,8},{12,14},{14,12},{1,3},{3,1},... | collective-permute-start | bytes 393224 | tf_op jit(solution)/shard_map/ppermute | solution.py:15
  62.3 5.7 %collective-permute-start.4 = (f32[64,512]{1,0:T(8,128)S(1)}, f32[64,512]{1,0:T(8,128)S(1)}, u32[]{:S(2)}, u32[]{:S(2)}) collective-permute-start(f32[64,512]{1,0:T(8,128)S(1)} %add.18), channel_id=1, source_target_pairs={{0,4},{2,6},{4,0},{6,2},{8,12},{10,14},{12,8},{14,10},{1,5},{3,7},... | collective-permute-start | bytes 393224 | tf_op jit(solution)/shard_map/ppermute | solution.py:15
  68.1 8.6 %collective-permute-start.5 = (f32[64,512]{1,0:T(8,128)S(1)}, f32[64,512]{1,0:T(8,128)S(1)}, u32[]{:S(2)}, u32[]{:S(2)}) collective-permute-start(f32[64,512]{1,0:T(8,128)S(1)} %add.19), channel_id=1, source_target_pairs={{0,8},{2,10},{4,12},{6,14},{8,0},{10,2},{12,4},{14,6},{1,9},{3,11}... | collective-permute-start | bytes 393224 | tf_op jit(solution)/shard_map/ppermute | solution.py:15
  78.9 5.0 %collective-permute-start.6 = (f32[64,512]{1,0:T(8,128)S(1)}, f32[64,512]{1,0:T(8,128)S(1)}, u32[]{:S(2)}, u32[]{:S(2)}) collective-permute-start(f32[64,512]{1,0:T(8,128)S(1)} %fusion.8), channel_id=1, source_target_pairs={{0,2},{2,0},{4,6},{6,4},{8,10},{10,8},{12,14},{14,12},{1,3},{3,1},... | collective-permute-start | bytes 393224 | tf_op jit(solution)/shard_map/ppermute | solution.py:15
  83.9 5.0 %collective-permute-start.7 = (f32[64,512]{1,0:T(8,128)S(1)}, f32[64,512]{1,0:T(8,128)S(1)}, u32[]{:S(2)}, u32[]{:S(2)}) collective-permute-start(f32[64,512]{1,0:T(8,128)S(1)} %add.21), channel_id=1, source_target_pairs={{0,4},{2,6},{4,0},{6,2},{8,12},{10,14},{12,8},{14,10},{1,5},{3,7},... | collective-permute-start | bytes 393224 | tf_op jit(solution)/shard_map/ppermute | solution.py:15
  89.0 7.3 %collective-permute-start.8 = (f32[64,512]{1,0:T(8,128)S(1)}, f32[64,512]{1,0:T(8,128)S(1)}, u32[]{:S(2)}, u32[]{:S(2)}) collective-permute-start(f32[64,512]{1,0:T(8,128)S(1)} %add.22), channel_id=1, source_target_pairs={{0,8},{2,10},{4,12},{6,14},{8,0},{10,2},{12,4},{14,6},{1,9},{3,11}... | collective-permute-start | bytes 393224 | tf_op jit(solution)/shard_map/ppermute | solution.py:15
